TPU v7x, 256 devices: a whole 4x4x8 slice. The times are simulated.
256 devices in a mesh: seq: 16 (over x, y), exp: 16 (over z, core).
Axes of the slice: x: 4, y: 4, z: 8, core: 2. Of those that a mesh axis runs over, the one named last changes fastest.
Arguments:
- tokens: bfloat16 [32, 1024, 1152], P('exp', 'seq'), may hold values from -80 to 80
- timesteps: int32 [32], P('exp'), may hold values from 0 to 63
- modulation: bfloat16 [64, 2, 1152], replicated, may hold values from -0.5 to 0.5
- routes: int32 [16, 1024, 2, 2], P('exp', 'seq'), may hold values from 0 to 15, all different within a row; in each aligned block of 128 rows (0 to 127, 128 to 255, ..., all dimensions but the last counted through in order) at most 17 rows name the same one
- gate_codes: int32 [32, 1024, 2], P('exp', 'seq'), may hold values from 1 to 16
- gate_weight: bfloat16 [16, 1152, 4608], P('exp', None, 'seq'), may hold values from -0.1875 to 0.1875
- up_weight: bfloat16 [16, 1152, 4608], P('exp', None, 'seq'), may hold values from -0.1875 to 0.1875
- down_weight: bfloat16 [16, 4608, 1152], P('exp', 'seq'), may hold values from -0.09375 to 0.09375
- cotangent: bfloat16 [32, 1024, 1152], P('exp', 'seq'), may hold values from -6 to 6
Outputs:
- grad_tokens: bfloat16 [32, 1024, 1152], P('exp', 'seq')
Inputs may be any that keep to these rules, and one draw needn't show every extreme that they name: `routes`: among the rows of one device (entries [g, p, i, :] with p in one block of 64 patches, all i) no expert is named more than 17 times, a bound that some block reaches.
All inputs are finite; a program needn't handle non-finite values.
Results may differ from a plain program's by a relative error of at most 0.015.
Values may be sent and summed in bfloat16 or wider, within the bound.
A program may use at most 192 MiB of HBM per device.

v0:
```python
import jax
import jax.numpy as jnp
from jax import lax
from jax.sharding import PartitionSpec as P


def in_one_piece(arrays, axis, split_dim, concat_dim, along):
    ends, at = ([], 0)
    for a in arrays[:-1]:
        at += a.shape[along]
        ends.append(at)
    both = jnp.concatenate(arrays, axis=along)
    return tuple(
        jnp.split(
            lax.all_to_all(both, axis, split_axis=split_dim, concat_axis=concat_dim, tiled=True),
            ends,
            axis=along,
        )
    )


def normalize_modulate(tokens_f, shift, scale):
    mean_square = jnp.mean(tokens_f * tokens_f, axis=-1, keepdims=True)
    return tokens_f / jnp.sqrt(mean_square + 1e-06) * (1.0 + scale) + shift


def per_device(
    tokens,
    timesteps,
    modulation,
    routes,
    gate_codes,
    gate_weight,
    up_weight,
    down_weight,
    cotangent,
):
    img_local, patch_local, feature_width = tokens.shape
    top_count = routes.shape[3]
    row_count = img_local * patch_local
    n_exp = lax.axis_size("exp")
    local_experts = gate_weight.shape[0]
    block_width = gate_weight.shape[2]
    expert_count = local_experts * n_exp
    capacity = top_count * row_count // expert_count + 1
    slot_count = expert_count * capacity
    level_count = modulation.shape[0]
    select = (timesteps[:, None] == jnp.arange(level_count, dtype=jnp.int32)[None, :]).astype(
        jnp.float32
    )
    table = jnp.dot(
        select,
        modulation.astype(jnp.float32).reshape(level_count, 2 * feature_width),
        precision=lax.Precision.HIGHEST,
    )
    table = jnp.broadcast_to(
        table[:, None, :], (img_local, patch_local, 2 * feature_width)
    ).reshape(row_count, 2 * feature_width)
    scale = table[:, :feature_width]
    shift = table[:, feature_width:]
    tokens_f = tokens.reshape(row_count, feature_width).astype(jnp.float32)
    pre, pullback = jax.vjp(lambda value: normalize_modulate(value, shift, scale), tokens_f)
    normed = pre.astype(jnp.bfloat16)
    codes = gate_codes.reshape(row_count, top_count).astype(jnp.float32)
    route_weight = codes / jnp.sum(codes, axis=-1, keepdims=True)
    flat_routes = jnp.transpose(routes[0], (1, 0, 2)).reshape(row_count * top_count)
    expert_hot = (
        flat_routes[:, None] == jnp.arange(expert_count, dtype=jnp.int32)[None, :]
    ).astype(jnp.int32)
    earlier = jnp.cumsum(expert_hot, axis=0) - expert_hot
    position = jnp.sum(earlier * expert_hot, axis=1)
    slot_ids = flat_routes * capacity + position
    slot_hot = (slot_ids[:, None] == jnp.arange(slot_count, dtype=jnp.int32)[None, :]).astype(
        jnp.float32
    )
    slot_hot = slot_hot.reshape(row_count, top_count, slot_count)
    member = jnp.sum(slot_hot, axis=1)
    weighted = jnp.sum(slot_hot * route_weight[:, :, None], axis=1)
    contract_tokens = (((0,), (0,)), ((), ()))
    send_rows = lax.dot_general(
        member.astype(jnp.bfloat16), normed, contract_tokens, preferred_element_type=jnp.float32
    ).astype(jnp.bfloat16)
    grads_f = cotangent.reshape(row_count, feature_width).astype(jnp.float32)
    send_grads = lax.dot_general(
        weighted, grads_f, contract_tokens, precision=lax.Precision.HIGHEST
    ).astype(jnp.bfloat16)
    send_rows = send_rows.reshape(n_exp, local_experts * capacity, feature_width)
    send_grads = send_grads.reshape(n_exp, local_experts * capacity, feature_width)
    arrived_rows, arrived_grads = in_one_piece((send_rows, send_grads), "exp", 0, 0, 1)

    def by_expert(arrived):
        shaped = arrived.reshape(n_exp, local_experts, capacity, feature_width)
        return jnp.transpose(shaped, (1, 0, 2, 3)).reshape(
            local_experts, n_exp * capacity, feature_width
        )

    rows_all = by_expert(arrived_rows)
    grads_all = by_expert(arrived_grads)
    weight_stack = jnp.stack([gate_weight, up_weight, jnp.swapaxes(down_weight, 1, 2)], axis=1)
    piece = lax.all_gather(weight_stack, "seq", axis=3, tiled=True)
    count = piece.shape[3] // block_width
    shaped = piece.reshape(local_experts, 3, feature_width, count, block_width)
    gate_part = shaped[0, 0]
    up_part = shaped[0, 1]
    down_part = shaped[0, 2]
    rows_in = rows_all[0]
    grads_in = grads_all[0]
    gate_pre = jnp.einsum("rd,dkf->krf", rows_in, gate_part, preferred_element_type=jnp.float32)
    up_pre = jnp.einsum("rd,dkf->krf", rows_in, up_part, preferred_element_type=jnp.float32)
    grad_hidden = jnp.einsum("rd,dkf->krf", grads_in, down_part, preferred_element_type=jnp.float32)
    sigma = jax.nn.sigmoid(gate_pre)
    silu_gate = gate_pre * sigma
    grad_gate_pre = (grad_hidden * up_pre * sigma * (1.0 + gate_pre * (1.0 - sigma))).astype(
        jnp.bfloat16
    )
    grad_up_pre = (grad_hidden * silu_gate).astype(jnp.bfloat16)
    back_term = jnp.einsum(
        "krf,dkf->krd", grad_gate_pre, gate_part, preferred_element_type=jnp.float32
    )
    back_term = back_term + jnp.einsum(
        "krf,dkf->krd", grad_up_pre, up_part, preferred_element_type=jnp.float32
    )
    back_term = back_term.astype(jnp.bfloat16).astype(jnp.float32)
    results = [jnp.sum(back_term, axis=0)]
    folded = jnp.stack(results)
    folded = folded.reshape(local_experts, n_exp, capacity, feature_width)
    slot_source = jnp.transpose(folded, (1, 0, 2, 3)).reshape(
        n_exp, local_experts * capacity, feature_width
    )
    slot_source = slot_source.astype(jnp.bfloat16)
    slot_backs = lax.all_to_all(slot_source, "exp", split_axis=0, concat_axis=0, tiled=True)
    slot_backs = slot_backs.reshape(slot_count, feature_width).astype(jnp.float32)
    grad_normed = jnp.dot(member, slot_backs, precision=lax.Precision.HIGHEST)
    grad_tokens = pullback(grad_normed)[0]
    return grad_tokens.astype(jnp.bfloat16).reshape(img_local, patch_local, feature_width)


def solution(mesh):
    in_specs = (
        P("exp", "seq", None),
        P("exp"),
        P(),
        P("exp", "seq", None, None),
        P("exp", "seq", None),
        P("exp", None, "seq"),
        P("exp", None, "seq"),
        P("exp", "seq", None),
        P("exp", "seq", None),
    )
    out_specs = P("exp", "seq", None)
    return jax.shard_map(
        per_device, mesh=mesh, in_specs=in_specs, out_specs=out_specs, check_vma=False
    )
```

profile of v0, /device:TPU:1, one launch (start us, length us, event | category | flops | bytes accessed | tf_op | source)
XLA Modules:
  0.0 319.6 jit_solution(1848872654035132093)
XLA Ops:
  6.6 3.1 pad_maximum_fusion
  9.7 0.8 copy.19
  10.5 0.1 eq.56
  10.8 0.7 convert_element_type.73
  11.5 0.7 convert_reduce_fusion.1
  12.2 1.1 fusion.22
  13.4 0.7 broadcast_multiply_fusion
  14.3 0.6 reduce-window.6
  14.9 0.2 slice_reduce_fusion
  15.2 0.1 reduce_sum.73
  15.6 0.7 convolution_convert_fusion
  16.2 0.2 reshape.138
  16.5 0.2 fusion.30
  16.8 0.2 fusion.21
  17.0 1.2 convolution_convert_fusion.1
  18.1 1.3 reshape.136
  19.4 0.3 pad_maximum_fusion.1
  19.7 47.3 %all_to_all.10 = bf16[16,34,1152]{2,1,0:T(8,128)(2,1)S(1)} all-to-all(bf16[16,34,1152]{2,1,0:T(8,128)(2,1)S(1)} %pad_maximum_fusion.1), channel_id=1, replica_groups=mesh['seq'=16,'exp'=16] {'exp'}, dimensions={0} | all-to-all | bytes 2506752 | tf_op jit(solution)/shard_map/all_to_all | solution.py:15
  67.1 0.2 fusion.37
  67.3 1.1 reshape.142
  68.4 0.2 reshape.143
  68.6 138.1 %all-gather.2.cloned.1.call-done = bf16[1,3,1152,4608]{2,3,1,0:T(8,128)(2,1)} async-done(((bf16[1,3,1152,288]{2,3,1,0:T(8,128)(2,1)}), bf16[1,3,1152,4608]{2,3,1,0:T(8,128)(2,1)}) %all-gather.2.cloned.1.call-update) | async-done | bytes 31850512 | tf_op jit(solution)/shard_map/all_gather | solution.py:100
  206.7 14.3 %fusion = f32[16,288,272]{1,2,0:T(8,128)} fusion(bf16[272,1152,1]{1,0,2:T(8,128)(2,1)} %reshape.142, bf16[1,3,1152,16,288]{2,4,3,1,0:T(8,128)(2,1)} %bitcast.127), kind=kOutput, calls=%fused_computation.4 | convolution fusion | flops 2887778304 | bytes 16257024 | tf_op jit(solution)/shard_map/rd,dkf->krf/dot_general | solution.py:110
  221.0 14.3 %fusion.3 = f32[16,288,272]{1,2,0:T(8,128)} fusion(bf16[272,1152,1]{1,0,2:T(8,128)(2,1)S(1)} %reshape.143, bf16[1,3,1152,16,288]{2,4,3,1,0:T(8,128)(2,1)} %bitcast.128), kind=kOutput, calls=%fused_computation.7 | convolution fusion | flops 2887778304 | bytes 16257024 | tf_op jit(solution)/shard_map/rd,dkf->krf/dot_general | solution.py:108
  235.3 24.0 %fusion.2 = f32[16,272,1152]{2,1,0:T(8,128)} fusion(bf16[1,3,1152,16,288]{2,4,3,1,0:T(8,128)(2,1)} %bitcast.129, f32[16,288,272]{1,2,0:T(8,128)} %fusion.3, f32[16,288,272]{1,2,0:T(8,128)} %fusion, bf16[272,1152,1]{1,0,2:T(8,128)(2,1)S(1)} %reshape.143), kind=kOutput, calls=%fused_computation.6 | convolution fusion | flops 5788090368 | bytes 55283712 | tf_op jit(solution)/shard_map/krf,dkf->krd/dot_general | solution.py:117
  259.3 17.7 %fusion.17 = bf16[272,1152]{1,0:T(8,128)(2,1)S(1)} fusion(f32[16,272,1152]{2,1,0:T(8,128)} %fusion.2, bf16[1,3,1152,16,288]{2,4,3,1,0:T(8,128)(2,1)} %bitcast.130, f32[16,288,272]{1,2,0:T(8,128)} %fusion.3, f32[16,288,272]{1,2,0:T(8,128)} %fusion), kind=kOutput, calls=%fused_computation.27 | convolution fusion | flops 2910025728 | bytes 44666880 | tf_op jit(solution)/shard_map/krf,dkf->krd/dot_general | solution.py:120
  277.0 1.1 convert_element_type.79
  278.1 7.9 %all-to-all-start.1 = ((bf16[16,17,1152]{2,1,0:T(8,128)(2,1)}), bf16[16,17,1152]{2,1,0:T(8,128)(2,1)S(1)}, u32[]{:S(2)}, u32[]{:S(2)}) async-start(bf16[16,17,1152]{2,1,0:T(8,128)(2,1)} %convert_element_type.79), calls=%async_computation.1 | async-start | bytes 1769472 | tf_op jit(solution)/shard_map/all_to_all | solution.py:131
  286.1 24.6 %all-to-all-done.1 = bf16[16,17,1152]{2,1,0:T(8,128)(2,1)S(1)} async-done(((bf16[16,17,1152]{2,1,0:T(8,128)(2,1)}), bf16[16,17,1152]{2,1,0:T(8,128)(2,1)S(1)}, u32[]{:S(2)}, u32[]{:S(2)}) %all-to-all-start.1) | async-done | bytes 626720 | tf_op jit(solution)/shard_map/all_to_all | solution.py:131
  310.7 0.2 reshape.139
  310.9 0.9 fusion.24
  311.8 0.9 fusion.20
  (37 shorter events, 1.1 us)
Async XLA Ops:
  6.5 9.0 %copy-start = (bf16[2,64,1152]{2,1,0:T(8,128)(2,1)S(1)}, bf16[2,64,1152]{2,1,0:T(8,128)(2,1)}, u32[]{:S(2)}) copy-start(bf16[2,64,1152]{2,1,0:T(8,128)(2,1)} %param.17) | copy-start | bytes 884740
  6.5 10.2 %copy-start.2 = (bf16[2,64,1152]{2,1,0:T(8,128)(2,1)S(1)}, bf16[2,64,1152]{2,1,0:T(8,128)(2,1)}, u32[]{:S(2)}) copy-start(bf16[2,64,1152]{2,1,0:T(8,128)(2,1)} %param.9) | copy-start | bytes 884740
  6.5 8.9 %copy-start.5 = (bf16[64,2,1152]{2,1,0:T(2,128)(2,1)S(1)}, bf16[64,2,1152]{2,1,0:T(2,128)(2,1)}, u32[]{:S(2)}) copy-start(bf16[64,2,1152]{2,1,0:T(2,128)(2,1)} %param.11) | copy-start | bytes 884740
  6.5 9.9 %copy-start.6 = (s32[2]{0:T(128)S(1)}, s32[2]{0:T(128)}, u32[]{:S(2)}) copy-start(s32[2]{0:T(128)} %param.10) | copy-start | bytes 28
  6.5 200.2 %all-gather.2.cloned.1.call-start = ((), (), s32[]{:S(2)}) async-start(), calls=%async_computation.2 | async-start | bytes 33841152 | tf_op jit(solution)/shard_map/all_gather | solution.py:100
  15.6 1.4 copy-start.3
  259.3 51.6 %copy-start.4 = (f32[128,272]{0,1:T(8,128)S(1)}, f32[128,272]{0,1:T(8,128)}, u32[]{:S(2)}) copy-start(f32[128,272]{0,1:T(8,128)} %copy-done.3) | copy-start | bytes 417796
  259.3 53.4 %copy-start.1 = (bf16[2,64,1152]{2,1,0:T(8,128)(2,1)S(1)}, bf16[2,64,1152]{2,1,0:T(8,128)(2,1)}, u32[]{:S(2)}) copy-start(bf16[2,64,1152]{2,1,0:T(8,128)(2,1)} %param.17) | copy-start | bytes 884740
  278.1 32.6 %all-to-all-start.1 = ((bf16[16,17,1152]{2,1,0:T(8,128)(2,1)}), bf16[16,17,1152]{2,1,0:T(8,128)(2,1)S(1)}, u32[]{:S(2)}, u32[]{:S(2)}) async-start(bf16[16,17,1152]{2,1,0:T(8,128)(2,1)} %convert_element_type.79), calls=%async_computation.1 | async-start | bytes 1769472 | tf_op jit(solution)/shard_map/all_to_all | solution.py:131
Sparse Core Ops, SparseCore 0:
  9.8 196.8 all-gather.1
where the time goes:
time: 320 us
  waiting for transfers between devices  163 us (51%)
  matrix products  73.1 us (23%)
  blocking collectives  47.3 us (15%)
  between operations  13.6 us (4%)
  other arithmetic  8.44 us (3%)
  starting transfers between devices  7.89 us (2%)
  local copies, waits for them, and re-layouts  6.47 us (2%)
    all_gather x1, waiting for transfers between devices, per_device(): piece = lax.all_gather(weight_stack, 'seq', axis=3, tiled=True)  138 us
    all_to_all x1, blocking collectives, in_one_piece(): lax.all_to_all(both, axis, split_axis=split_dim, concat_axis=concat_dim,...  47.3 us
    all_to_all x1, waiting for transfers between devices, per_device(): lax.all_to_all(slot_source, 'exp', split_axis=0, concat_axis=0, tiled=True)  24.6 us
    dot_general x1, matrix products, per_device(): jnp.einsum('krf,dkf->krd', grad_gate_pre, gate_part, preferred_element_ty...  24 us
    dot_general x1, matrix products, per_device(): jnp.einsum('krf,dkf->krd', grad_up_pre, up_part, preferred_element_type=j...  17.7 us
    dot_general x1, matrix products, per_device(): jnp.einsum('rd,dkf->krf', grads_in, down_part, preferred_element_type=jnp...  14.3 us
    dot_general x1, matrix products, per_device(): jnp.einsum('rd,dkf->krf', rows_in, gate_part, preferred_element_type=jnp....  14.3 us
    all_to_all x1, starting transfers between devices, per_device(): lax.all_to_all(slot_source, 'exp', split_axis=0, concat_axis=0, tiled=True)  7.86 us
  transfers between devices with their start and end apart: 2, of which 2 were waited for; matrix products, arithmetic and copies ran while one was open for 4% of the time, Pallas kernels for 0%

commit v1 on v0

--- a/solution.py
+++ b/solution.py
@@ -97,7 +97,9 @@
     rows_all = by_expert(arrived_rows)
     grads_all = by_expert(arrived_grads)
     weight_stack = jnp.stack([gate_weight, up_weight, jnp.swapaxes(down_weight, 1, 2)], axis=1)
-    piece = lax.all_gather(weight_stack, "seq", axis=3, tiled=True)
+    piece = jnp.concatenate(
+        lax.all_to_all(jnp.stack([weight_stack] * lax.axis_size("seq")), "seq", 0, 0), axis=3
+    )
     count = piece.shape[3] // block_width
     shaped = piece.reshape(local_experts, 3, feature_width, count, block_width)
     gate_part = shaped[0, 0]

time: 320 us -> 810 us (2.53)
  waiting for transfers between devices: 163 us -> 661 us
  blocking collectives: 47.3 us -> 0 us
  local copies, waits for them, and re-layouts: 6.47 us -> 41.3 us
  between operations: 13.6 us -> 0.2 us
  starting transfers between devices: 7.89 us -> 20.3 us
    all_to_all x0 -> x2, waiting for transfers between devices: none -> 637 us  [the longest x1 602 us: per_device(): lax.all_to_all(jnp.stack([weight_stack] * lax.axis_size('seq')), 'seq', 0...]
    all_gather x1 -> x0, waiting for transfers between devices: 138 us -> none  [per_device(): piece = lax.all_gather(weight_stack, 'seq', axis=3, tiled=True)]
    all_to_all x1 -> x0, blocking collectives: 47.3 us -> none  [in_one_piece(): lax.all_to_all(both, axis, split_axis=split_dim, concat_axis=concat_dim,...]
    all_to_all x0 -> x1, local copies, waits for them, and re-layouts: none -> 22 us  [per_device(): lax.all_to_all(jnp.stack([weight_stack] * lax.axis_size('seq')), 'seq', 0...]
    all_to_all x0 -> x2, starting transfers between devices: none -> 16.8 us  [the longest x1 9.97 us: in_one_piece(): lax.all_to_all(both, axis, split_axis=split_dim, concat_axis=concat_dim,...]
    another operation x1 -> x2, local copies, waits for them, and re-layouts: 0.01 us -> 10.4 us  [the longest x1 10.4 us: per_device(): jnp.stack([weight_stack] * lax.axis_size('seq'))]
  transfers between devices with their start and end apart: 2 -> 3, of which waited for: 2 -> 3; matrix products, arithmetic and copies ran while one was open for 4% -> 1% of each run, Pallas kernels for 0% -> 0%
where the time goes in v1:
time: 810 us; the launch traced here: 806 us
  waiting for transfers between devices  661 us (82%)
  matrix products  73.9 us (9%)
  local copies, waits for them, and re-layouts  41.3 us (5%)
  starting transfers between devices  20.3 us (3%)
  other arithmetic  9.28 us (1%)
    all_to_all x1, waiting for transfers between devices, per_device(): lax.all_to_all(jnp.stack([weight_stack] * lax.axis_size('seq')), 'seq', 0...  602 us
    all_to_all x1, waiting for transfers between devices, in_one_piece(): lax.all_to_all(both, axis, split_axis=split_dim, concat_axis=concat_dim,...  34.9 us
    all_to_all x1, waiting for transfers between devices, per_device(): lax.all_to_all(slot_source, 'exp', split_axis=0, concat_axis=0, tiled=True)  24.5 us
    dot_general x1, matrix products, per_device(): jnp.einsum('krf,dkf->krd', grad_gate_pre, gate_part, preferred_element_ty...  24 us
    all_to_all x1, local copies, waits for them, and re-layouts, per_device(): lax.all_to_all(jnp.stack([weight_stack] * lax.axis_size('seq')), 'seq', 0...  22 us
    dot_general x1, matrix products, per_device(): jnp.einsum('krf,dkf->krd', grad_up_pre, up_part, preferred_element_type=j...  17.9 us
  transfers between devices with their start and end apart: 3, of which 3 were waited for; matrix products, arithmetic and copies ran while one was open for 1% of the time, Pallas kernels for 0%

profile of v1, /device:TPU:1, one launch (start us, length us, event | category | flops | bytes accessed | tf_op | source)
XLA Modules:
  0.0 806.1 jit_solution(5502850105059017408)
XLA Ops:
  0.0 0.7 convert_reduce_fusion.1
  0.7 0.7 convert_element_type.73
  1.4 0.7 broadcast_multiply_fusion
  2.1 0.8 copy.28
  3.3 1.1 fusion.22
  4.6 0.6 reduce-window.6
  5.8 1.0 copy.35
  6.9 0.6 convolution_convert_fusion
  7.8 0.9 fusion.30
  8.7 1.2 fusion.21
  9.9 1.1 convolution_convert_fusion.1
  11.0 1.3 reshape.139
  12.3 1.4 pad_maximum_fusion
  13.8 10.0 %all-to-all-start.1 = ((bf16[16,34,1152]{2,1,0:T(8,128)(2,1)}), bf16[16,34,1152]{2,1,0:T(8,128)(2,1)}, u32[]{:S(2)}, u32[]{:S(2)}) async-start(bf16[16,34,1152]{2,1,0:T(8,128)(2,1)} %pad_maximum_fusion), calls=%async_computation.1 | async-start | bytes 2949120 | tf_op jit(solution)/shard_map/all_to_all | solution.py:15
  23.7 1.8 maximum_bitcast_fusion
  25.5 34.9 %all-to-all-done.1 = bf16[16,34,1152]{2,1,0:T(8,128)(2,1)} async-done(((bf16[16,34,1152]{2,1,0:T(8,128)(2,1)}), bf16[16,34,1152]{2,1,0:T(8,128)(2,1)}, u32[]{:S(2)}, u32[]{:S(2)}) %all-to-all-start.1) | async-done | bytes 1253408 | tf_op jit(solution)/shard_map/all_to_all | solution.py:15
  60.4 10.4 %stack.17 = bf16[16,1,3,1152,288]{3,4,2,1,0:T(8,128)(2,1)} broadcast(bf16[3,1152,288]{1,2,0:T(8,128)(2,1)S(1)} %maximum_bitcast_fusion), dimensions={2,3,4} | broadcast | bytes 33841152 | tf_op jit(solution)/shard_map/stack | solution.py:101
  70.8 6.8 all-to-all-start
  77.6 1.7 fusion.37
  79.3 1.1 reshape.145
  80.4 0.2 reshape.146
  80.6 601.8 %all-to-all-done = bf16[16,1,3,1152,288]{3,4,2,1,0:T(8,128)(2,1)} async-done(((bf16[16,1,3,1152,288]{3,4,2,1,0:T(8,128)(2,1)}), bf16[16,1,3,1152,288]{3,4,2,1,0:T(8,128)(2,1)}, u32[]{:S(2)}, u32[]{:S(2)}) %all-to-all-start) | async-done | bytes 31850528 | tf_op jit(solution)/shard_map/all_to_all | solution.py:101
  682.4 22.0 %copy.38 = bf16[16,1,3,1152,288]{3,4,0,2,1:T(8,128)(2,1)} copy(bf16[16,1,3,1152,288]{3,4,2,1,0:T(8,128)(2,1)} %all-to-all-done) | data formatting | bytes 63700992 | tf_op jit(solution)/shard_map/all_to_all | solution.py:101
  704.4 14.3 %fusion = f32[16,288,272]{1,2,0:T(8,128)} fusion(bf16[272,1152,1]{1,0,2:T(8,128)(2,1)S(1)} %copy-done.5, bf16[1,3,1152,16,288]{2,4,3,1,0:T(8,128)(2,1)} %bitcast.123), kind=kOutput, calls=%fused_computation.5 | convolution fusion | flops 2887778304 | bytes 16257024 | tf_op jit(solution)/shard_map/rd,dkf->krf/dot_general | solution.py:112
  718.7 14.2 %fusion.3 = f32[16,288,272]{1,2,0:T(8,128)} fusion(bf16[272,1152,1]{1,0,2:T(8,128)(2,1)S(1)} %reshape.146, bf16[1,3,1152,16,288]{2,4,3,1,0:T(8,128)(2,1)} %bitcast.124), kind=kOutput, calls=%fused_computation.8 | convolution fusion | flops 2887778304 | bytes 16257024 | tf_op jit(solution)/shard_map/rd,dkf->krf/dot_general | solution.py:110
  732.9 24.0 %fusion.2 = f32[16,272,1152]{2,1,0:T(8,128)} fusion(bf16[1,3,1152,16,288]{2,4,3,1,0:T(8,128)(2,1)} %bitcast.125, f32[16,288,272]{1,2,0:T(8,128)} %fusion.3, f32[16,288,272]{1,2,0:T(8,128)} %fusion, bf16[272,1152,1]{1,0,2:T(8,128)(2,1)S(1)} %reshape.146), kind=kOutput, calls=%fused_computation.7 | convolution fusion | flops 5788090368 | bytes 55283712 | tf_op jit(solution)/shard_map/krf,dkf->krd/dot_general | solution.py:119
  756.9 17.9 %fusion.17 = bf16[272,1152]{1,0:T(8,128)(2,1)S(1)} fusion(f32[16,272,1152]{2,1,0:T(8,128)} %fusion.2, bf16[1,3,1152,16,288]{2,4,3,1,0:T(8,128)(2,1)} %bitcast.126, f32[16,288,272]{1,2,0:T(8,128)} %fusion.3, f32[16,288,272]{1,2,0:T(8,128)} %fusion), kind=kOutput, calls=%fused_computation.28 | convolution fusion | flops 2910025728 | bytes 44666880 | tf_op jit(solution)/shard_map/krf,dkf->krd/dot_general | solution.py:122
  774.8 1.1 convert_element_type.79
  775.9 3.5 all-to-all-start.2
  779.5 24.5 %all-to-all-done.2 = bf16[16,17,1152]{2,1,0:T(8,128)(2,1)S(1)} async-done(((bf16[16,17,1152]{2,1,0:T(8,128)(2,1)}), bf16[16,17,1152]{2,1,0:T(8,128)(2,1)S(1)}, u32[]{:S(2)}, u32[]{:S(2)}) %all-to-all-start.2) | async-done | bytes 626720 | tf_op jit(solution)/shard_map/all_to_all | solution.py:133
  804.3 0.9 fusion.24
  805.1 0.9 fusion.20
  (37 shorter events, 1.9 us)
Async XLA Ops:
  0.0 6.9 copy-start
  6.9 3.0 copy-start.3
  13.8 46.6 %all-to-all-start.1 = ((bf16[16,34,1152]{2,1,0:T(8,128)(2,1)}), bf16[16,34,1152]{2,1,0:T(8,128)(2,1)}, u32[]{:S(2)}, u32[]{:S(2)}) async-start(bf16[16,34,1152]{2,1,0:T(8,128)(2,1)} %pad_maximum_fusion), calls=%async_computation.1 | async-start | bytes 2949120 | tf_op jit(solution)/shard_map/all_to_all | solution.py:15
  70.8 611.6 %all-to-all-start = ((bf16[16,1,3,1152,288]{3,4,2,1,0:T(8,128)(2,1)}), bf16[16,1,3,1152,288]{3,4,2,1,0:T(8,128)(2,1)}, u32[]{:S(2)}, u32[]{:S(2)}) async-start(bf16[16,1,3,1152,288]{3,4,2,1,0:T(8,128)(2,1)} %stack.17), calls=%async_computation | async-start | bytes 63700992 | tf_op jit(solution)/shard_map/all_to_all | solution.py:101
  80.6 623.8 %copy-start.5 = (bf16[272,1152,1]{1,0,2:T(8,128)(2,1)S(1)}, bf16[272,1152,1]{1,0,2:T(8,128)(2,1)}, u32[]{:S(2)}) copy-start(bf16[272,1152,1]{1,0,2:T(8,128)(2,1)} %reshape.145) | copy-start | bytes 1880068
  756.9 47.4 %copy-start.2 = (bf16[2,64,1152]{2,1,0:T(8,128)(2,1)S(1)}, bf16[2,64,1152]{2,1,0:T(8,128)(2,1)}, u32[]{:S(2)}) copy-start(bf16[2,64,1152]{2,1,0:T(8,128)(2,1)} %param.9) | copy-start | bytes 884740
  756.9 47.4 %copy-start.4 = (f32[128,272]{0,1:T(8,128)S(1)}, f32[128,272]{0,1:T(8,128)}, u32[]{:S(2)}) copy-start(f32[128,272]{0,1:T(8,128)} %copy-done.3) | copy-start | bytes 417796
  756.9 49.2 %copy-start.1 = (bf16[2,64,1152]{2,1,0:T(8,128)(2,1)S(1)}, bf16[2,64,1152]{2,1,0:T(8,128)(2,1)}, u32[]{:S(2)}) copy-start(bf16[2,64,1152]{2,1,0:T(8,128)(2,1)} %param.17) | copy-start | bytes 884740
  775.9 28.1 %all-to-all-start.2 = ((bf16[16,17,1152]{2,1,0:T(8,128)(2,1)}), bf16[16,17,1152]{2,1,0:T(8,128)(2,1)S(1)}, u32[]{:S(2)}, u32[]{:S(2)}) async-start(bf16[16,17,1152]{2,1,0:T(8,128)(2,1)} %convert_element_type.79), calls=%async_computation.2 | async-start | bytes 1769472 | tf_op jit(solution)/shard_map/all_to_all | solution.py:133
